TPU v7x, 128 devices: a whole 4x4x4 slice. The times are simulated.
128 devices in a mesh: ctx: 32 (over x, z, core), own: 4 (over y).
Axes of the slice: x: 4, y: 4, z: 4, core: 2. Of those that a mesh axis runs over, the one named last changes fastest.
Arguments:
- query_proj: bfloat16 [16384, 8192], P(('ctx', 'own')), may hold values from -6 to 6
- key_proj: bfloat16 [16384, 8192], P(('ctx', 'own')), may hold values from -6 to 6
- value_proj: bfloat16 [16384, 8192], P(('ctx', 'own')), may hold values from -6 to 6
- short_taps: float32 [3, 7, 512], P(None, None, 'own'), may hold values from -2 to 2
- long_taps: float32 [128, 512], P(None, 'own'), may hold values from -0.5 to 0.5
- decay_rate: float32 [8, 8192], P(None, 'own'), may hold values from 3.0517579e-06 to 0.03
- residues: float32 [8, 8192], P(None, 'own'), may hold values from -2 to 2
- grad_out: bfloat16 [16384, 8192], P(('ctx', 'own')), may hold values from -6 to 6
Outputs:
- layer_out: bfloat16 [16384, 8192], P(('ctx', 'own'))
- grad_query: bfloat16 [16384, 8192], P(('ctx', 'own'))
- grad_key: bfloat16 [16384, 8192], P(('ctx', 'own'))
- grad_value: bfloat16 [16384, 8192], P(('ctx', 'own'))
- grad_long_taps: float32 [128, 512], P(None, 'own')
All inputs are finite; a program needn't handle non-finite values.
Results may differ from a plain program's by a relative error of at most 0.02.
Values may be sent and summed in bfloat16 or wider, within the bound.
No kernel may reach another device: no remote copies, remote signals or barrier semaphores. Data moves between devices by JAX's collectives and lax.ppermute only.
A program may use at most 256 MiB of HBM per device.

v0:
```python
import math
import jax
import jax.numpy as jnp
from jax import lax
from jax.sharding import PartitionSpec as P

CPG = 16
exact_mode = lax.Precision.HIGHEST


def from_behind(value, axis, steps):
    count = lax.axis_size(axis)
    leading, last = (max(0, -steps), min(count, count - steps))
    return lax.ppermute(value, axis, [(source, source + steps) for source in range(leading, last)])


def carried_in(x, axis, combine, identity, reverse):
    size, index = (lax.axis_size(axis), lax.axis_index(axis))
    everything = jax.tree.map(
        lambda part, kind: lax.all_gather(part.astype(kind), axis), x, (jnp.bfloat16, jnp.bfloat16)
    )
    start = jax.tree.map(
        lambda part, zero: jnp.broadcast_to(jnp.asarray(zero, part.dtype), part.shape), x, identity
    )

    def hop(k, before):
        at = size - 1 - k if reverse else k
        reached = at > index if reverse else at < index
        new = combine(
            before, jax.tree.map(lambda part, own: part[at].astype(own.dtype), everything, x)
        )
        return jax.tree.map(lambda a, b: jnp.where(reached, a, b), new, before)

    return lax.fori_loop(0, size, hop, start)


def tables(row_count):
    bin_count = row_count + 1
    freq_index = jnp.arange(bin_count, dtype=jnp.int32)[:, None]
    place_index = jnp.arange(row_count, dtype=jnp.int32)[None, :]
    phase_index = freq_index * place_index % (2 * row_count)
    angle_all = phase_index.astype(jnp.float32) * (math.pi / row_count)
    cos_fwd = jnp.cos(angle_all)
    sin_fwd = jnp.sin(angle_all)
    at_edge = jnp.logical_or(freq_index == 0, freq_index == row_count)
    weight_bin = jnp.where(at_edge, 1.0, 2.0).astype(jnp.float32) / (2.0 * row_count)
    cos_inv = jnp.transpose(cos_fwd * weight_bin)
    sin_inv = jnp.transpose(sin_fwd * weight_bin)
    parity = (1 - 2 * (freq_index % 2)).astype(jnp.float32)
    return (cos_fwd, sin_fwd, cos_inv, sin_inv, parity)


def transform(table_set, rows_in):
    values = rows_in.astype(jnp.float32)
    real_part = jnp.dot(
        table_set[0], values, precision=exact_mode, preferred_element_type=jnp.float32
    )
    imag_part = -jnp.dot(
        table_set[1], values, precision=exact_mode, preferred_element_type=jnp.float32
    )
    return (real_part, imag_part)


def restore(table_set, real_part, imag_part):
    first = jnp.dot(
        table_set[2], real_part, precision=exact_mode, preferred_element_type=jnp.float32
    )
    return first - jnp.dot(
        table_set[3], imag_part, precision=exact_mode, preferred_element_type=jnp.float32
    )


def featurize(rim_part, main_rows, taps_chan):
    joined = jnp.concatenate([rim_part, main_rows], axis=0).astype(jnp.float32)
    row_count = main_rows.shape[0]
    tap_count = taps_chan.shape[0]
    summed = jnp.zeros(main_rows.shape, jnp.float32)
    for offset in range(tap_count):
        first_row = tap_count - 1 - offset
        summed = summed + taps_chan[offset][None, :] * joined[first_row : first_row + row_count]
    return summed.astype(jnp.bfloat16)


def unfeaturize(main_rows, rim_part, taps_chan):
    joined = jnp.concatenate([main_rows, rim_part], axis=0).astype(jnp.float32)
    row_count = main_rows.shape[0]
    tap_count = taps_chan.shape[0]
    summed = jnp.zeros(main_rows.shape, jnp.float32)
    for offset in range(tap_count):
        summed = summed + taps_chan[offset][None, :] * joined[offset : offset + row_count]
    return summed.astype(jnp.bfloat16)


def spread(spectrum):
    bin_count, group_count = spectrum.shape
    return jnp.broadcast_to(spectrum[:, :, None], (bin_count, group_count, CPG)).reshape(
        bin_count, group_count * CPG
    )


def modal_weight(decay, resid):
    return resid * jnp.sqrt(-jnp.expm1(-2.0 * decay))


def pole_rows(coeff, decay, lag_rows, scaling):
    summed = jnp.zeros((lag_rows.shape[0], decay.shape[1]), jnp.float32)
    for pole in range(decay.shape[0]):
        summed = summed + (coeff[pole] * scaling[pole])[None, :] * jnp.exp(
            -decay[pole][None, :] * lag_rows[:, None]
        )
    return summed


def pole_states(decay, lag_rows, field):
    states = []
    for pole in range(decay.shape[0]):
        states.append(jnp.sum(jnp.exp(-decay[pole][None, :] * lag_rows[:, None]) * field, axis=0))
    return jnp.stack(states)


def shards(query_proj, key_proj, value_proj, short_taps, long_taps, decay_rate, residues, grad_out):
    row_count, chan_count = query_proj.shape
    rim_rows = short_taps.shape[1] - 1
    table_set = tables(row_count)
    parity = table_set[4]
    lag_index = jnp.arange(row_count, dtype=jnp.float32)
    weight = modal_weight(decay_rate, residues)
    head_rows = pole_rows(weight, decay_rate, lag_index, jnp.ones_like(weight))
    head_re, head_im = transform(table_set, head_rows)
    taps_re, taps_im = transform(table_set, long_taps)
    head_all, taps_all, decay_all, resid_all, short_all = (
        lax.all_gather(jnp.stack([head_re, head_im]), "own", axis=2, tiled=True),
        lax.all_gather(jnp.stack([taps_re, taps_im]), "own", axis=2, tiled=True),
        lax.all_gather(decay_rate, "own", axis=1, tiled=True),
        lax.all_gather(residues, "own", axis=1, tiled=True),
        lax.all_gather(short_taps, "own", axis=2, tiled=True),
    )
    head_re, head_im = (head_all[0], head_all[1])
    edge_re, edge_im = (spread(taps_all[0]), spread(taps_all[1]))
    tap_count = short_all.shape[1]
    group_count = short_all.shape[2]
    short_chan = jnp.broadcast_to(
        short_all[:, :, :, None], (3, tap_count, group_count, CPG)
    ).reshape(3, tap_count, group_count * CPG)
    weight_all = modal_weight(decay_all, resid_all)
    block_rate = decay_all * row_count

    def chain_pair(earlier_pair, later_pair):
        return (
            earlier_pair[0] + later_pair[0],
            jnp.exp(-block_rate * later_pair[0]) * earlier_pair[1] + later_pair[1],
        )

    identity = (jnp.zeros((), jnp.float32), jnp.zeros_like(block_rate))
    one_block = jnp.ones((), jnp.float32)
    rim_set = from_behind(
        (
            query_proj[row_count - rim_rows :],
            key_proj[row_count - rim_rows :],
            value_proj[row_count - rim_rows :],
        ),
        ("ctx", "own"),
        1,
    )
    query_feat = featurize(rim_set[0], query_proj, short_chan[0])
    key_feat = featurize(rim_set[1], key_proj, short_chan[1])
    value_feat = featurize(rim_set[2], value_proj, short_chan[2])
    product = (key_feat.astype(jnp.float32) * value_feat.astype(jnp.float32)).astype(jnp.bfloat16)
    earlier = from_behind(product, ("ctx", "own"), 1)
    product_float = product.astype(jnp.float32)
    block_state = pole_states(decay_all, row_count - 1 - lag_index, product_float)
    state_in = carried_in((one_block, block_state), ("ctx", "own"), chain_pair, identity, False)[1]
    prev_re, prev_im = transform(table_set, earlier)
    own_re, own_im = transform(table_set, product)
    own_re = parity * own_re
    own_im = parity * own_im
    win_re = prev_re + own_re
    win_im = prev_im + own_im
    out_re = win_re * edge_re - win_im * edge_im + own_re * head_re - own_im * head_im
    out_im = win_re * edge_im + win_im * edge_re + own_re * head_im + own_im * head_re
    near_part = restore(table_set, parity * out_re, parity * out_im)
    far_part = pole_rows(weight_all, decay_all, lag_index + 1.0, state_in)
    long_conv = near_part + far_part
    layer_out = (query_feat.astype(jnp.float32) * long_conv).astype(jnp.bfloat16)
    grad_float = grad_out.astype(jnp.float32)
    grad_conv = (grad_float * query_feat.astype(jnp.float32)).astype(jnp.bfloat16)
    grad_qfeat = (grad_float * long_conv).astype(jnp.bfloat16)
    next_grad = from_behind(grad_conv, ("ctx", "own"), -1)
    conv_float = grad_conv.astype(jnp.float32)
    back_state = pole_states(decay_all, lag_index, conv_float)
    state_after = carried_in((one_block, back_state), ("ctx", "own"), chain_pair, identity, True)[1]
    cur_re, cur_im = transform(table_set, grad_conv)
    nxt_re, nxt_im = transform(table_set, next_grad)
    gwin_re = cur_re + parity * nxt_re
    gwin_im = cur_im + parity * nxt_im
    back_re = gwin_re * edge_re + gwin_im * edge_im + cur_re * head_re + cur_im * head_im
    back_im = gwin_im * edge_re - gwin_re * edge_im + cur_im * head_re - cur_re * head_im
    near_back = restore(table_set, back_re, back_im)
    far_back = pole_rows(weight_all, decay_all, row_count - lag_index, state_after)
    grad_prod = near_back + far_back
    grad_kfeat = (grad_prod * value_feat.astype(jnp.float32)).astype(jnp.bfloat16)
    grad_vfeat = (grad_prod * key_feat.astype(jnp.float32)).astype(jnp.bfloat16)
    back_rims = from_behind(
        (grad_qfeat[:rim_rows], grad_kfeat[:rim_rows], grad_vfeat[:rim_rows]), ("ctx", "own"), -1
    )
    grad_query = unfeaturize(grad_qfeat, back_rims[0], short_chan[0])
    grad_key = unfeaturize(grad_kfeat, back_rims[1], short_chan[1])
    grad_value = unfeaturize(grad_vfeat, back_rims[2], short_chan[2])
    corr_re = parity * (cur_re * win_re + cur_im * win_im)
    corr_im = parity * (cur_im * win_re - cur_re * win_im)
    bin_count = corr_re.shape[0]
    all_groups = chan_count // CPG
    corr_re = corr_re.reshape(bin_count, all_groups, CPG).sum(axis=2)
    corr_im = corr_im.reshape(bin_count, all_groups, CPG).sum(axis=2)
    seq_total = row_count * lax.axis_size("ctx") * lax.axis_size("own")
    scale_taps = 1.0 / math.sqrt(seq_total * CPG)
    partial_taps = (
        jnp.dot(table_set[2], corr_re, precision=exact_mode, preferred_element_type=jnp.float32)
        - jnp.dot(table_set[3], corr_im, precision=exact_mode, preferred_element_type=jnp.float32)
    ) * scale_taps
    summed_taps = lax.psum(partial_taps, ("ctx", "own"))
    own_groups = all_groups // lax.axis_size("own")
    grad_taps = lax.dynamic_slice_in_dim(
        summed_taps, lax.axis_index("own") * own_groups, own_groups, 1
    )
    return (layer_out, grad_query, grad_key, grad_value, grad_taps)


def solution(mesh):
    placed = (
        P(("ctx", "own"), None),
        P(("ctx", "own"), None),
        P(("ctx", "own"), None),
        P(None, None, "own"),
        P(None, "own"),
        P(None, "own"),
        P(None, "own"),
        P(("ctx", "own"), None),
    )
    return jax.shard_map(
        shards,
        mesh=mesh,
        in_specs=placed,
        out_specs=(
            P(("ctx", "own"), None),
            P(("ctx", "own"), None),
            P(("ctx", "own"), None),
            P(("ctx", "own"), None),
            P(None, "own"),
        ),
        check_vma=False,
    )
```

profile of v0, /device:TPU:18, one launch (start us, length us, event | category | flops | bytes accessed | tf_op | source)
XLA Modules:
  0.0 1164.0 jit_solution(342298592889918397)
XLA Ops:
  9.7 3.2 collective-permute-start.2
  14.4 1.9 collective-permute-start.1
  18.0 2.8 collective-permute-start
  21.9 12.6 %all_gather.27 = f32[3,7,512]{2,1,0:T(8,128)S(1)} all-gather(f32[3,7,128]{2,1,0:T(8,128)} %param.15), channel_id=1, replica_groups=mesh['ctx'=32,'own'=4] {'own'}, dimensions={2}, use_global_device_ids=true | all-gather | bytes 53760 | tf_op jit(solution)/shard_map/all_gather | solution.py:136
  34.6 1.9 slice_negate_fusion.15
  36.5 12.5 %all_gather.31 = f32[8,8192]{1,0:T(8,128)S(1)} all-gather(f32[8,2048]{1,0:T(8,128)} %param.17), channel_id=1, replica_groups=mesh['ctx'=32,'own'=4] {'own'}, dimensions={1}, use_global_device_ids=true | all-gather | bytes 327680 | tf_op jit(solution)/shard_map/all_gather | solution.py:134
  56.3 1.8 maximum_convert_fusion
  61.8 24.6 %fusion.62 = (bf16[8192]{0:T(1024)(128)(2,1)}, bf16[8192]{0:T(1024)(128)(2,1)}, bf16[8192]{0:T(1024)(128)(2,1)}, bf16[8192]{0:T(1024)(128)(2,1)}, bf16[8192]{0:T...) fusion(f32[8192]{0:T(1024)S(1)} %bitcast.146, ...), kind=kLoop, calls=%fused_computation.101 | loop fusion | flops 104726528 | bytes 101876224 | tf_op jit(solution)/shard_map/reduce_sum | solution.py:117
  86.5 3.0 collective-permute-start.3
  89.6 3.7 convolution_bitcast_fusion
  93.3 3.6 fusion.105
  96.9 2.1 convolution_negate_fusion.1
  99.1 2.4 fusion.5
  101.4 2.2 convolution_multiply_fusion.1
  103.7 28.1 %collective-permute-done.3 = bf16[128,8192]{1,0:T(8,128)(2,1)S(1)} collective-permute-done((bf16[128,8192]{1,0:T(8,128)(2,1)S(1)}, bf16[128,8192]{1,0:T(8,128)(2,1)S(1)}, u32[]{:S(2)}, u32[]{:S(2)}) %collective-permute-start.3) | collective-permute-done | bytes 2097184 | tf_op jit(solution)/shard_map/ppermute | solution.py:14
  131.7 2.3 convolution_add_fusion
  134.1 2.5 fusion.6
  136.6 16.6 %subtract_multiply_fusion = (f32[129,8192]{1,0:T(8,128)}, f32[129,8192]{1,0:T(8,128)}, f32[129,8192]{1,0:T(8,128)}) fusion(f32[129,8192]{1,0:T(8,128)S(1)} %fusion.6, f32[129,8192]{1,0:T(8,128)S(1)} %convolution_negate_fusion.1, f32[129,8192]{1,0:T(8,128)S(1)} %convolution_add_fusion, f32[129]{0:T(256)S(1)} %copy-done.77, ...), kind=kOutput, calls=%fused_computation.46 | convolution fusion | flops 1631880960 | bytes 27460100 | tf_op jit(solution)/shard_map/dot_general | solution.py:55
  153.2 7.6 copy.36
  160.8 5.2 bitcast_reduce_fusion
  166.0 7.6 copy.35
  173.7 5.2 bitcast_reduce_fusion.1
  181.6 3.2 pad_maximum_fusion
  187.4 12.7 %all_gather.28 = f32[2,129,512]{2,1,0:T(8,128)S(1)} all-gather(f32[2,129,128]{2,1,0:T(8,128)S(1)} %pad_maximum_fusion.1), channel_id=1, replica_groups=mesh['ctx'=32,'own'=4] {'own'}, dimensions={2}, use_global_device_ids=true | all-gather | bytes 660480 | tf_op jit(solution)/shard_map/all_gather | solution.py:133
  203.0 5.1 broadcast_in_dim.218
  208.1 8.0 copy.28
  216.1 4.0 broadcast_in_dim.216
  220.1 8.1 copy.26
  228.3 72.0 %all-reduce = bf16[128]{0:T(256)(128)(2,1)} all-reduce(bf16[128]{0:T(256)(128)(2,1)S(1)} %dynamic-update-slice), channel_id=1, replica_groups=mesh['ctx'=32,'own'=4] {'ctx','own'}, use_global_device_ids=true, to_apply=%add | all-reduce | flops 128 | bytes 512
  300.3 2.9 collective-permute-start.5
  303.3 69.3 %all_gather.30 = f32[8,8192]{1,0:T(8,128)S(1)} all-gather(f32[8,2048]{1,0:T(8,128)S(1)} %copy-done.52), channel_id=1, replica_groups=mesh['ctx'=32,'own'=4] {'own'}, dimensions={1}, use_global_device_ids=true | all-gather | bytes 327680 | tf_op jit(solution)/shard_map/all_gather | solution.py:135
  380.2 7.5 fusion.3
  387.8 6.0 fusion.4
  393.8 39.3 %all-reduce.3.cloned.1.call-done = f32[128,512]{1,0:T(8,128)} async-done(((f32[128,512]{1,0:T(8,128)}), f32[128,512]{1,0:T(8,128)}) %all-reduce.3.cloned.1.call-update) | async-done | bytes 262160 | tf_op jit(solution)/shard_map/psum | solution.py:221
  434.6 20.2 %fusion.32 = f32[128,8192]{1,0:T(8,128)} fusion(f32[129,8192]{1,0:T(8,128)} %copy-done.3, f32[129,8192]{1,0:T(8,128)} %copy-done.4, f32[129,8192]{1,0:T(8,128)} %copy-done.6, f32[129,8192]{1,0:T(8,128)} %copy.28, f32[129,8192]{1,0:T(8,128)} %copy-done.5, f32[129,8192]{1,0:T(8,128)} %copy.26, f32[2,129,8192]{2,1,0:T(8,128)} %all-gather.4.cloned.1.call-done, ...), kind=kOutput, calls=%fused_computation.71 | convolution fusion | flops 1631897472 | bytes 38011912 | tf_op jit(solution)/shard_map/dot_general | solution.py:65
  454.8 19.2 %fusion.16 = f32[128,8192]{1,0:T(8,128)} fusion(f32[129,8192]{1,0:T(8,128)} %copy-done.2, f32[129,8192]{1,0:T(8,128)} %get-tuple-element.478, f32[129,8192]{1,0:T(8,128)} %fusion.3, f32[129,8192]{1,0:T(8,128)} %copy.28, f32[129,8192]{1,0:T(8,128)S(1)} %copy-done.7, f32[129,8192]{1,0:T(8,128)} %copy.26, f32[2,129,8192]{2,1,0:T(8,128)} %all-gather.4.cloned.1.call-done, ...), kind=kOutput, calls=%fused_computation.55 | convolution fusion | flops 1630840704 | bytes 38011396 | tf_op jit(solution)/shard_map/dot_general | solution.py:65
  474.0 301.8 %while.33 = (s32[]{:T(128)}, f32[8,8192]{1,0:T(8,128)S(1)}, s32[]{:T(128)}, bf16[128]{0:T(256)(128)(2,1)S(1)}, f32[8,8192]{1,0:T(8,128)S(1)}, /*index=5*/bf16[12...) while((s32[]{:T(128)}, f32[8,8192]{1,0:T(8,128)S(1)}, s32[]{:T(128)}, ...), condition=%wide.region_19.20_spmd.clone, body=%wide.region_18.19_spmd.clone.sunk | while | flops 393225 | bytes 917701 | solution.py:34
  776.0 303.6 %while.32 = (s32[]{:T(128)}, f32[8,8192]{1,0:T(8,128)S(1)}, s32[]{:T(128)}, bf16[128]{0:T(256)(128)(2,1)S(1)}, f32[8,8192]{1,0:T(8,128)S(1)}, /*index=5*/bf16[128,8,8192]{2,1,0:T(8,128)(2,1)}, s32[]{:T(128)}, s32[]{:T(128)}) while((s32[]{:T(128)}, f32[8,8192]{1,0:T(8,128)S(1)}, s32[]{:T(128)}, bf16[128]{0:T(256)(128)(2,1)S(1)}, ...), condition=%wide.region_9.10_spmd.clone, body=%wide.region_8.9_spmd.clone.sunk | while | flops 393221 | bytes 917639 | solution.py:34
  1080.5 19.6 %fusion.8 = f32[128,8192]{1,0:T(8,128)} fusion(f32[128,8192]{1,0:T(8,128)} %fusion.32, f32[129,8192]{1,0:T(8,128)} %copy-done.3, f32[129,8192]{1,0:T(8,128)} %copy-done.4, f32[129,8192]{1,0:T(8,128)} %copy-done.6, f32[129,8192]{1,0:T(8,128)} %copy.26, f32[129,8192]{1,0:T(8,128)} %copy-done.5, f32[129,8192]{1,0:T(8,128)} %copy.28, ...), kind=kOutput, calls=%fused_computation.35 | convolution fusion | flops 1658111872 | bytes 42731016 | tf_op jit(solution)/shard_map/dot_general | solution.py:68
  1100.0 5.8 fusion.45
  1105.8 2.3 collective-permute-start.4
  1108.1 18.6 %fusion.7 = f32[128,8192]{1,0:T(8,128)} fusion(f32[128,8192]{1,0:T(8,128)} %fusion.16, f32[129,8192]{1,0:T(8,128)} %get-tuple-element.478, f32[129,8192]{1,0:T(8,128)S(1)} %bitcast.138, f32[129,8192]{1,0:T(8,128)} %fusion.4, f32[129,8192]{1,0:T(8,128)} %copy.28, f32[129,8192]{1,0:T(8,128)} %fusion.3, f32[129,8192]{1,0:T(8,128)} %copy.26, ...), kind=kOutput, calls=%fused_computation.33 | convolution fusion | flops 1657055104 | bytes 42730500 | tf_op jit(solution)/shard_map/dot_general | solution.py:68
  1126.7 4.5 fusion.42
  1131.3 3.5 collective-permute-start.6
  1134.8 5.6 collective-permute-start.7
  1141.0 4.5 fusion.78
  1146.3 4.4 fusion.64
  1151.6 4.4 fusion.71
  (821 shorter events, 471.0 us)
Async XLA Ops:
  8.0 178.3 %copy-start = (f32[128,128]{1,0:T(8,128)S(1)}, f32[128,128]{1,0:T(8,128)}, u32[]{:S(2)}) copy-start(f32[128,128]{1,0:T(8,128)} %param.16) | copy-start | bytes 196612
  8.0 425.1 %all-reduce.3.cloned.1.call-start = ((), (), s32[]{:S(2)}) async-start(), calls=%async_computation.3 | async-start | bytes 524288 | tf_op jit(solution)/shard_map/psum | solution.py:221
  9.7 50.1 %collective-permute-start.2 = (bf16[6,8192]{1,0:T(8,128)(2,1)}, bf16[6,8192]{1,0:T(8,128)(2,1)}, u32[]{:S(2)}, u32[]{:S(2)}) collective-permute-start(bf16[6,8192]{1,0:T(8,128)(2,1)} %slice.600), channel_id=1, source_target_pairs={{0,1},{1,2},{2,3},{3,4},{4,5},{5,6},{6,7},{7,8},{8,9},{9,10},{10,1... | collective-permute-start | bytes 294920 | tf_op jit(solution)/shard_map/ppermute | solution.py:14
  14.4 43.6 %collective-permute-start.1 = (bf16[6,8192]{1,0:T(8,128)(2,1)}, bf16[6,8192]{1,0:T(8,128)(2,1)}, u32[]{:S(2)}, u32[]{:S(2)}) collective-permute-start(bf16[6,8192]{1,0:T(8,128)(2,1)} %slice.578), channel_id=1, source_target_pairs={{0,1},{1,2},{2,3},{3,4},{4,5},{5,6},{6,7},{7,8},{8,9},{9,10},{10,1... | collective-permute-start | bytes 294920 | tf_op jit(solution)/shard_map/ppermute | solution.py:14
  18.0 38.3 %collective-permute-start = (bf16[6,8192]{1,0:T(8,128)(2,1)}, bf16[6,8192]{1,0:T(8,128)(2,1)}, u32[]{:S(2)}, u32[]{:S(2)}) collective-permute-start(bf16[6,8192]{1,0:T(8,128)(2,1)} %slice.556), channel_id=1, source_target_pairs={{0,1},{1,2},{2,3},{3,4},{4,5},{5,6},{6,7},{7,8},{8,9},{9,10},{10,1... | collective-permute-start | bytes 294920 | tf_op jit(solution)/shard_map/ppermute | solution.py:14
  50.3 11.1 copy-start.16
  50.6 10.9 copy-start.20
  51.4 10.1 copy-start.14
  51.7 9.8 copy-start.18
  61.7 27.8 %copy-start.81 = (f32[1,2048]{1,0:T(1,128)S(1)}, f32[1,2048]{1,0:T(1,128)}, u32[]{:S(2)}) copy-start(f32[1,2048]{1,0:T(1,128)} %get-tuple-element.449) | copy-start | bytes 24580
  61.7 27.8 %copy-start.82 = (f32[1,2048]{1,0:T(1,128)S(1)}, f32[1,2048]{1,0:T(1,128)}, u32[]{:S(2)}) copy-start(f32[1,2048]{1,0:T(1,128)} %get-tuple-element.450) | copy-start | bytes 24580
  61.7 27.8 %copy-start.83 = (f32[1,2048]{1,0:T(1,128)S(1)}, f32[1,2048]{1,0:T(1,128)}, u32[]{:S(2)}) copy-start(f32[1,2048]{1,0:T(1,128)} %get-tuple-element.451) | copy-start | bytes 24580
  61.8 27.8 %copy-start.84 = (f32[1,2048]{1,0:T(1,128)S(1)}, f32[1,2048]{1,0:T(1,128)}, u32[]{:S(2)}) copy-start(f32[1,2048]{1,0:T(1,128)} %get-tuple-element.452) | copy-start | bytes 24580
  61.8 27.8 %copy-start.85 = (f32[1,2048]{1,0:T(1,128)S(1)}, f32[1,2048]{1,0:T(1,128)}, u32[]{:S(2)}) copy-start(f32[1,2048]{1,0:T(1,128)} %get-tuple-element.453) | copy-start | bytes 24580
  61.8 27.8 %copy-start.86 = (f32[1,2048]{1,0:T(1,128)S(1)}, f32[1,2048]{1,0:T(1,128)}, u32[]{:S(2)}) copy-start(f32[1,2048]{1,0:T(1,128)} %get-tuple-element.454) | copy-start | bytes 24580
  61.8 27.8 %copy-start.87 = (f32[1,2048]{1,0:T(1,128)S(1)}, f32[1,2048]{1,0:T(1,128)}, u32[]{:S(2)}) copy-start(f32[1,2048]{1,0:T(1,128)} %get-tuple-element.455) | copy-start | bytes 24580
  61.8 27.8 %copy-start.88 = (f32[1,2048]{1,0:T(1,128)S(1)}, f32[1,2048]{1,0:T(1,128)}, u32[]{:S(2)}) copy-start(f32[1,2048]{1,0:T(1,128)} %get-tuple-element.456) | copy-start | bytes 24580
  86.5 45.3 %collective-permute-start.3 = (bf16[128,8192]{1,0:T(8,128)(2,1)S(1)}, bf16[128,8192]{1,0:T(8,128)(2,1)S(1)}, u32[]{:S(2)}, u32[]{:S(2)}) collective-permute-start(bf16[128,8192]{1,0:T(8,128)(2,1)S(1)} %get-tuple-element.404), channel_id=1, source_target_pairs={{0,1},{1,2},{2,3},{3,4},{4,5},{5,6},{6,7},{7,8},{8,9},{9,10},{10,1... | collective-permute-start | bytes 6291464 | tf_op jit(solution)/shard_map/ppermute | solution.py:14
  99.1 37.5 %copy-start.2 = (f32[129,8192]{1,0:T(8,128)}, f32[129,8192]{1,0:T(8,128)S(1)}, u32[]{:S(2)}) copy-start(f32[129,8192]{1,0:T(8,128)S(1)} %convolution_negate_fusion.1) | copy-start | bytes 12681220
  101.4 32.6 %copy-start.3 = (f32[129,8192]{1,0:T(8,128)}, f32[129,8192]{1,0:T(8,128)S(1)}, u32[]{:S(2)}) copy-start(f32[129,8192]{1,0:T(8,128)S(1)} %fusion.5) | copy-start | bytes 12681220
  103.6 30.4 %copy-start.4 = (f32[129,8192]{1,0:T(8,128)}, f32[129,8192]{1,0:T(8,128)S(1)}, u32[]{:S(2)}) copy-start(f32[129,8192]{1,0:T(8,128)S(1)} %convolution_multiply_fusion.1) | copy-start | bytes 12681220
  136.6 16.6 %copy-start.6 = (f32[129,8192]{1,0:T(8,128)}, f32[129,8192]{1,0:T(8,128)S(1)}, u32[]{:S(2)}) copy-start(f32[129,8192]{1,0:T(8,128)S(1)} %fusion.6) | copy-start | bytes 12681220
  181.5 253.1 %all-gather.4.cloned.1.call-start = ((), (), s32[]{:S(2)}) async-start(), calls=%async_computation | async-start | bytes 11141120 | tf_op jit(solution)/shard_map/all_gather | solution.py:132
  184.8 289.2 %all-gather.8.cloned.1.call-start = ((), (), s32[]{:S(2)}) async-start(), calls=%async_computation.2 | async-start | bytes 16908288 | tf_op jit(solution)/shard_map/all_gather | solution.py:20
  186.2 589.8 %all-gather.6.cloned.1.call-start = ((), (), s32[]{:S(2)}) async-start(), calls=%async_computation.1 | async-start | bytes 16908288 | tf_op jit(solution)/shard_map/all_gather | solution.py:20
  220.1 83.1 %copy-start.52 = (f32[8,2048]{1,0:T(8,128)S(1)}, f32[8,2048]{1,0:T(8,128)}, u32[]{:S(2)}) copy-start(f32[8,2048]{1,0:T(8,128)} %param.18) | copy-start | bytes 196612
  220.1 153.6 %copy-start.13 = (f32[8,8192]{1,0:T(8,128)S(1)}, f32[8,8192]{1,0:T(8,128)}, u32[]{:S(2)}) copy-start(f32[8,8192]{1,0:T(8,128)} %copy-done.12) | copy-start | bytes 786436
  220.1 159.0 %copy-start.69 = (bf16[8192]{0:T(1024)(128)(2,1)S(1)}, bf16[8192]{0:T(1024)(128)(2,1)}, u32[]{:S(2)}) copy-start(bf16[8192]{0:T(1024)(128)(2,1)} %get-tuple-element.377) | copy-start | bytes 49156
  300.3 79.9 %collective-permute-start.5 = (bf16[128,8192]{1,0:T(8,128)(2,1)S(1)}, bf16[128,8192]{1,0:T(8,128)(2,1)}, u32[]{:S(2)}, u32[]{:S(2)}) collective-permute-start(bf16[128,8192]{1,0:T(8,128)(2,1)S(1)} %get-tuple-element.402), channel_id=1, source_target_pairs={{1,0},{2,1},{3,2},{4,3},{5,4},{6,5},{7,6},{8,7},{9,8},{10,9},{11,1... | collective-permute-start | bytes 6291464 | tf_op jit(solution)/shard_map/ppermute | solution.py:14
  387.8 46.8 %copy-start.80 = (f32[129]{0:T(256)S(1)}, f32[129]{0:T(256)}, u32[]{:S(2)}) copy-start(f32[129]{0:T(256)} %fusion.150) | copy-start | bytes 1552
  434.6 20.2 %copy-start.7 = (f32[129,8192]{1,0:T(8,128)S(1)}, f32[129,8192]{1,0:T(8,128)}, u32[]{:S(2)}) copy-start(f32[129,8192]{1,0:T(8,128)} %fusion.4) | copy-start | bytes 12681220
  454.8 19.2 %copy-start.89 = (bf16[128]{0:T(256)(128)(2,1)S(1)}, bf16[128]{0:T(256)(128)(2,1)}, u32[]{:S(2)}) copy-start(bf16[128]{0:T(256)(128)(2,1)} %all-reduce) | copy-start | bytes 772
  775.9 304.5 %copy-start.54 = (f32[1,8192]{1,0:T(1,128)S(1)}, f32[1,8192]{1,0:T(1,128)}, u32[]{:S(2)}) copy-start(f32[1,8192]{1,0:T(1,128)} %copy-done.53) | copy-start | bytes 98308
  775.9 304.5 %copy-start.56 = (f32[1,8192]{1,0:T(1,128)S(1)}, f32[1,8192]{1,0:T(1,128)}, u32[]{:S(2)}) copy-start(f32[1,8192]{1,0:T(1,128)} %copy-done.55) | copy-start | bytes 98308
  775.9 304.5 %copy-start.58 = (f32[1,8192]{1,0:T(1,128)S(1)}, f32[1,8192]{1,0:T(1,128)}, u32[]{:S(2)}) copy-start(f32[1,8192]{1,0:T(1,128)} %copy-done.57) | copy-start | bytes 98308
  775.9 304.5 %copy-start.60 = (f32[1,8192]{1,0:T(1,128)S(1)}, f32[1,8192]{1,0:T(1,128)}, u32[]{:S(2)}) copy-start(f32[1,8192]{1,0:T(1,128)} %copy-done.59) | copy-start | bytes 98308
  775.9 304.5 %copy-start.62 = (f32[1,8192]{1,0:T(1,128)S(1)}, f32[1,8192]{1,0:T(1,128)}, u32[]{:S(2)}) copy-start(f32[1,8192]{1,0:T(1,128)} %copy-done.61) | copy-start | bytes 98308
  775.9 304.5 %copy-start.64 = (f32[1,8192]{1,0:T(1,128)S(1)}, f32[1,8192]{1,0:T(1,128)}, u32[]{:S(2)}) copy-start(f32[1,8192]{1,0:T(1,128)} %copy-done.63) | copy-start | bytes 98308
  775.9 304.5 %copy-start.66 = (f32[1,8192]{1,0:T(1,128)S(1)}, f32[1,8192]{1,0:T(1,128)}, u32[]{:S(2)}) copy-start(f32[1,8192]{1,0:T(1,128)} %copy-done.65) | copy-start | bytes 98308
  776.0 304.5 %copy-start.68 = (f32[1,8192]{1,0:T(1,128)S(1)}, f32[1,8192]{1,0:T(1,128)}, u32[]{:S(2)}) copy-start(f32[1,8192]{1,0:T(1,128)} %copy-done.67) | copy-start | bytes 98308
  776.0 304.5 %copy-start.91 = (f32[128]{0:T(128)S(1)}, f32[128]{0:T(128)}, u32[]{:S(2)}) copy-start(f32[128]{0:T(128)} %iota_add_fusion) | copy-start | bytes 1540
  776.0 332.1 %slice-start = ((s8[4456448]{0:T(1024)(128)(4,1)}), s8[262144]{0:T(1024)(128)(4,1)S(1)}, s32[]{:S(2)}) async-start(s8[4456448]{0:T(1024)(128)(4,1)} %bitcast.137), calls=%async_computation.4 | async-start | bytes 524288
  1080.4 27.7 %slice-start.1 = ((s8[4456448]{0:T(1024)(128)(4,1)}), s8[4194304]{0:T(1024)(128)(4,1)S(1)}, s32[]{:S(2)}) async-start(s8[4456448]{0:T(1024)(128)(4,1)} %bitcast.137), calls=%async_computation.5 | async-start | bytes 8388608
  1105.8 34.6 %collective-permute-start.4 = (bf16[6,8192]{1,0:T(8,128)(2,1)S(1)}, bf16[6,8192]{1,0:T(8,128)(2,1)S(1)}, u32[]{:S(2)}, u32[]{:S(2)}) collective-permute-start(bf16[6,8192]{1,0:T(8,128)(2,1)S(1)} %slice.766), channel_id=1, source_target_pairs={{1,0},{2,1},{3,2},{4,3},{5,4},{6,5},{7,6},{8,7},{9,8},{10,9},{11,1... | collective-permute-start | bytes 294920 | tf_op jit(solution)/shard_map/ppermute | solution.py:14
  1131.2 9.7 copy-start.17
  1131.2 9.7 copy-start.21
  1131.3 19.5 %collective-permute-start.6 = (bf16[6,8192]{1,0:T(8,128)(2,1)S(1)}, bf16[6,8192]{1,0:T(8,128)(2,1)S(1)}, u32[]{:S(2)}, u32[]{:S(2)}) collective-permute-start(bf16[6,8192]{1,0:T(8,128)(2,1)S(1)} %slice.774), channel_id=1, source_target_pairs={{1,0},{2,1},{3,2},{4,3},{5,4},{6,5},{7,6},{8,7},{9,8},{10,9},{11,1... | collective-permute-start | bytes 294920 | tf_op jit(solution)/shard_map/ppermute | solution.py:14
  1134.8 10.6 collective-permute-start.7
  (60 other events, 314.7 us)
Sparse Core Ops, SparseCore 0:
  181.6 251.4 all-reduce.2
Sparse Core Ops, SparseCore 1:
  184.9 93.0 all-gather.3
  281.0 99.9 all-gather.7
  384.6 83.4 all-gather.5
where the time goes:
time: 1180 us; the launch traced here: 1160 us
  other arithmetic  358 us (30%)
  local copies, waits for them, and re-layouts  215 us (18%)
  blocking collectives  179 us (15%)
  loops' own time  171 us (14%)
  matrix products  130 us (11%)
  waiting for transfers between devices  67.5 us (6%)
  starting transfers between devices  25.5 us (2%)
  between operations  18.2 us (2%)
    select_n x256, other arithmetic, hop(): return jax.tree.map(lambda a, b: jnp.where(reached, a, b), new, before)  283 us
    another operation x2, loops' own time, carried_in(): return lax.fori_loop(0, size, hop, start)  171 us
    dynamic_slice x256, local copies, waits for them, and re-layouts, hop(): part[at].astype(own.dtype)  152 us
    unnamed x1, blocking collectives  72 us
    all_gather x1, blocking collectives, shards(): lax.all_gather(residues, 'own', axis=1, tiled=True)  69.3 us
    dot_general x2, matrix products, restore(): jnp.dot(table_set[2], real_part, precision=exact_mode, preferred_element_...  39.4 us
    psum x1, waiting for transfers between devices, shards(): summed_taps = lax.psum(partial_taps, ('ctx', 'own'))  39.3 us
    dot_general x2, matrix products, restore(): jnp.dot(table_set[3], imag_part, precision=exact_mode, preferred_element_...  38.1 us
  transfers between devices with their start and end apart: 12, of which 2 were waited for; matrix products, arithmetic and copies ran while one was open for 32% of the time, Pallas kernels for 0%

commit v1 on v0

--- a/solution.py
+++ b/solution.py
@@ -218,7 +218,7 @@
         jnp.dot(table_set[2], corr_re, precision=exact_mode, preferred_element_type=jnp.float32)
         - jnp.dot(table_set[3], corr_im, precision=exact_mode, preferred_element_type=jnp.float32)
     ) * scale_taps
-    summed_taps = lax.psum(partial_taps, ("ctx", "own"))
+    summed_taps = jnp.sum(lax.all_gather(partial_taps, ("ctx", "own")), axis=0)
     own_groups = all_groups // lax.axis_size("own")
     grad_taps = lax.dynamic_slice_in_dim(
         summed_taps, lax.axis_index("own") * own_groups, own_groups, 1

time: 1180 us -> 1100 us (0.932)
  waiting for transfers between devices: 67.5 us -> 4.72 us
    all_gather x1, blocking collectives: 69.3 us -> 13.8 us  [shards(): lax.all_gather(residues, 'own', axis=1, tiled=True)]
    all_gather x1, blocking collectives: 12.7 us -> 60.1 us  [shards(): lax.all_gather(jnp.stack([taps_re, taps_im]), 'own', axis=2, tiled=True)]
    psum x1 -> x0, waiting for transfers between devices: 39.3 us -> none  [shards(): summed_taps = lax.psum(partial_taps, ('ctx', 'own'))]
    ppermute x8, waiting for transfers between devices: 28.1 us -> 4.63 us  [from_behind(): lax.ppermute(value, axis, [(source, source + steps) for source in range(l...]
    reduce_sum x0 -> x1, other arithmetic: none -> 12 us  [shards(): summed_taps = jnp.sum(lax.all_gather(partial_taps, ('ctx', 'own')), axis=0)]
  transfers between devices with their start and end apart: 12 -> 12, of which waited for: 2 -> 2; matrix products, arithmetic and copies ran while one was open for 32% -> 62% of each run, Pallas kernels for 0% -> 0%
where the time goes in v1:
time: 1100 us; the launch traced here: 1090 us
  other arithmetic  361 us (33%)
  local copies, waits for them, and re-layouts  213 us (19%)
  loops' own time  174 us (16%)
  blocking collectives  170 us (15%)
  matrix products  122 us (11%)
  starting transfers between devices  24.7 us (2%)
  between operations  15.8 us (1%)
    select_n x256, other arithmetic, hop(): return jax.tree.map(lambda a, b: jnp.where(reached, a, b), new, before)  284 us
    another operation x2, loops' own time, carried_in(): return lax.fori_loop(0, size, hop, start)  174 us
    dynamic_slice x256, local copies, waits for them, and re-layouts, hop(): part[at].astype(own.dtype)  150 us
    unnamed x1, blocking collectives  69.3 us
    all_gather x1, blocking collectives, shards(): lax.all_gather(jnp.stack([taps_re, taps_im]), 'own', axis=2, tiled=True)  60.1 us
    dot_general x2, matrix products, restore(): jnp.dot(table_set[3], imag_part, precision=exact_mode, preferred_element_...  38.7 us
    dot_general x2, matrix products, restore(): jnp.dot(table_set[2], real_part, precision=exact_mode, preferred_element_...  37.1 us
    ppermute x8, starting transfers between devices, from_behind(): lax.ppermute(value, axis, [(source, source + steps) for source in range(l...  24.6 us
  transfers between devices with their start and end apart: 12, of which 2 were waited for; matrix products, arithmetic and copies ran while one was open for 62% of the time, Pallas kernels for 0%

profile of v1, /device:TPU:18, one launch (start us, length us, event | category | flops | bytes accessed | tf_op | source)
XLA Modules:
  0.0 1086.1 jit_solution(2475167646171333675)
XLA Ops:
  9.5 2.6 fusion.105
  12.2 2.6 convolution_bitcast_fusion
  18.0 3.2 collective-permute-start.2
  22.8 1.9 collective-permute-start.1
  25.4 2.8 collective-permute-start
  28.3 12.7 %all_gather.33 = f32[3,7,512]{2,1,0:T(8,128)S(1)} all-gather(f32[3,7,128]{2,1,0:T(8,128)S(1)} %copy-done.70), channel_id=1, replica_groups=mesh['ctx'=32,'own'=4] {'own'}, dimensions={2}, use_global_device_ids=true | all-gather | bytes 53760 | tf_op jit(solution)/shard_map/all_gather | solution.py:136
  48.7 14.2 %all_gather.37 = f32[8,8192]{1,0:T(8,128)S(1)} all-gather(f32[8,2048]{1,0:T(8,128)S(1)} %copy-done.14), channel_id=1, replica_groups=mesh['ctx'=32,'own'=4] {'own'}, dimensions={1}, use_global_device_ids=true | all-gather | bytes 327680 | tf_op jit(solution)/shard_map/all_gather | solution.py:134
  64.8 1.6 maximum_convert_fusion.1
  68.1 24.1 %fusion.62 = (bf16[8192]{0:T(1024)(128)(2,1)S(1)}, bf16[8192]{0:T(1024)(128)(2,1)S(1)}, bf16[8192]{0:T(1024)(128)(2,1)S(1)}, bf16[8192]{0:T(1024)(128)(2,1)S(1)}...) fusion(f32[8192]{0:T(1024)S(1)} %bitcast.148, ...), kind=kLoop, calls=%fused_computation.101 | loop fusion | flops 104726528 | bytes 101876224 | tf_op jit(solution)/shard_map/reduce_sum | solution.py:117
  94.9 13.8 %all_gather.36 = f32[8,8192]{1,0:T(8,128)S(1)} all-gather(f32[8,2048]{1,0:T(8,128)S(1)} %copy-done.53), channel_id=1, replica_groups=mesh['ctx'=32,'own'=4] {'own'}, dimensions={1}, use_global_device_ids=true | all-gather | bytes 327680 | tf_op jit(solution)/shard_map/all_gather | solution.py:135
  109.9 3.9 collective-permute-start.3
  113.8 60.1 %all_gather.34 = f32[2,129,512]{2,1,0:T(8,128)S(1)} all-gather(f32[2,129,128]{2,1,0:T(8,128)S(1)} %pad_maximum_fusion.1), channel_id=1, replica_groups=mesh['ctx'=32,'own'=4] {'own'}, dimensions={2}, use_global_device_ids=true | all-gather | bytes 660480 | tf_op jit(solution)/shard_map/all_gather | solution.py:133
  174.8 2.0 copy.25
  176.8 2.0 copy.27
  178.8 5.0 broadcast_in_dim.218
  183.8 8.3 copy.28
  192.1 5.1 broadcast_in_dim.216
  197.2 8.2 copy.26
  205.6 69.3 %all-reduce = bf16[128]{0:T(256)(128)(2,1)S(1)} all-reduce(bf16[128]{0:T(256)(128)(2,1)S(1)} %dynamic-update-slice), channel_id=1, replica_groups=mesh['ctx'=32,'own'=4] {'ctx','own'}, use_global_device_ids=true, to_apply=%add | all-reduce | flops 128 | bytes 512
  275.4 3.2 collective-permute-start.5
  278.6 2.1 convolution_negate_fusion.1
  280.8 2.4 fusion.5
  283.1 2.2 convolution_multiply_fusion.1
  285.4 5.5 convolution_add_fusion
  290.9 5.6 fusion.6
  296.5 6.6 subtract_multiply_fusion
  303.1 7.6 copy.36
  310.7 7.7 copy.35
  318.4 5.4 bitcast_reduce_fusion.1
  324.7 1.8 bitcast_reduce_fusion
  329.5 7.3 fusion.3
  336.8 6.0 fusion.4
  342.8 18.9 %fusion.32 = f32[128,8192]{1,0:T(8,128)} fusion(f32[129,8192]{1,0:T(8,128)} %copy-done.3, f32[129,8192]{1,0:T(8,128)} %copy-done.4, f32[129,8192]{1,0:T(8,128)} %copy-done.6, f32[129,8192]{1,0:T(8,128)} %copy.28, f32[129,8192]{1,0:T(8,128)} %copy-done.5, f32[129,8192]{1,0:T(8,128)} %copy.26, f32[2,129,8192]{2,1,0:T(8,128)} %all-gather.6.cloned.1.call-done, ...), kind=kOutput, calls=%fused_computation.71 | convolution fusion | flops 1631897472 | bytes 38011912 | tf_op jit(solution)/shard_map/dot_general | solution.py:65
  361.7 18.2 %fusion.16 = f32[128,8192]{1,0:T(8,128)} fusion(f32[129,8192]{1,0:T(8,128)} %copy-done.2, f32[129,8192]{1,0:T(8,128)} %get-tuple-element.478, f32[129,8192]{1,0:T(8,128)S(1)} %copy-done.9, f32[129,8192]{1,0:T(8,128)} %copy.28, f32[129,8192]{1,0:T(8,128)} %fusion.4, f32[129,8192]{1,0:T(8,128)} %copy.26, f32[2,129,8192]{2,1,0:T(8,128)} %all-gather.6.cloned.1.call-done, ...), kind=kOutput, calls=%fused_computation.55 | convolution fusion | flops 1630840704 | bytes 38011396 | tf_op jit(solution)/shard_map/dot_general | solution.py:65
  379.9 304.8 %while.33 = (s32[]{:T(128)}, f32[8,8192]{1,0:T(8,128)S(1)}, s32[]{:T(128)}, bf16[128]{0:T(256)(128)(2,1)S(1)}, f32[8,8192]{1,0:T(8,128)S(1)}, /*index=5*/bf16[12...) while((s32[]{:T(128)}, f32[8,8192]{1,0:T(8,128)S(1)}, s32[]{:T(128)}, ...), condition=%wide.region_19.20_spmd.clone, body=%wide.region_18.19_spmd.clone.sunk | while | flops 393225 | bytes 917701 | solution.py:34
  684.7 303.6 %while.32 = (s32[]{:T(128)}, f32[8,8192]{1,0:T(8,128)S(1)}, s32[]{:T(128)}, bf16[128]{0:T(256)(128)(2,1)S(1)}, f32[8,8192]{1,0:T(8,128)S(1)}, /*index=5*/bf16[128,8,8192]{2,1,0:T(8,128)(2,1)}, s32[]{:T(128)}, s32[]{:T(128)}) while((s32[]{:T(128)}, f32[8,8192]{1,0:T(8,128)S(1)}, s32[]{:T(128)}, bf16[128]{0:T(256)(128)(2,1)S(1)}, ...), condition=%wide.region_9.10_spmd.clone, body=%wide.region_8.9_spmd.clone.sunk | while | flops 393221 | bytes 917639 | solution.py:34
  988.8 20.0 %fusion.8 = f32[128,8192]{1,0:T(8,128)} fusion(f32[128,8192]{1,0:T(8,128)} %fusion.32, f32[129,8192]{1,0:T(8,128)} %copy-done.3, f32[129,8192]{1,0:T(8,128)} %copy-done.4, f32[129,8192]{1,0:T(8,128)} %copy-done.6, f32[129,8192]{1,0:T(8,128)} %copy.26, f32[129,8192]{1,0:T(8,128)} %copy-done.5, f32[129,8192]{1,0:T(8,128)} %copy.28, ...), kind=kOutput, calls=%fused_computation.35 | convolution fusion | flops 1658111872 | bytes 42731016 | tf_op jit(solution)/shard_map/dot_general | solution.py:68
  1008.8 5.8 fusion.45
  1014.6 2.8 collective-permute-start.4
  1017.8 18.7 %fusion.7 = f32[128,8192]{1,0:T(8,128)} fusion(f32[128,8192]{1,0:T(8,128)} %fusion.16, f32[129,8192]{1,0:T(8,128)} %get-tuple-element.478, f32[129,8192]{1,0:T(8,128)S(1)} %bitcast.139, f32[129,8192]{1,0:T(8,128)} %fusion.4, f32[129,8192]{1,0:T(8,128)} %copy.28, f32[129,8192]{1,0:T(8,128)} %fusion.3, f32[129,8192]{1,0:T(8,128)} %copy.26, ...), kind=kOutput, calls=%fused_computation.33 | convolution fusion | flops 1657055104 | bytes 42730500 | tf_op jit(solution)/shard_map/dot_general | solution.py:68
  1036.5 4.5 fusion.42
  1041.0 3.6 collective-permute-start.6
  1044.7 3.1 collective-permute-start.7
  1048.3 3.3 collective-permute-done.7
  1052.9 4.7 fusion.78
  1057.7 4.5 fusion.64
  1062.2 4.5 fusion.71
  1066.7 12.0 %reduce_sum.189 = f32[128,512]{1,0:T(8,128)S(1)} reduce(f32[128,128,512]{2,1,0:T(8,128)} %bitcast.142, f32[]{:T(128)} %constant.137.clone.1), dimensions={0}, to_apply=%region_22.23 | reduce | flops 8323072 | bytes 33816580 | tf_op jit(solution)/shard_map/reduce_sum | solution.py:221
  (782 shorter events, 464.5 us)
Async XLA Ops:
  7.2 101.5 %copy-start = (f32[128,128]{1,0:T(8,128)S(1)}, f32[128,128]{1,0:T(8,128)}, u32[]{:S(2)}) copy-start(f32[128,128]{1,0:T(8,128)} %param.16) | copy-start | bytes 196612
  7.2 335.6 %all-gather.6.cloned.1.call-start = ((), (), s32[]{:S(2)}) async-start(), calls=%async_computation | async-start | bytes 11141120 | tf_op jit(solution)/shard_map/all_gather | solution.py:132
  14.8 9.9 copy-start.11
  14.8 13.4 %copy-start.70 = (f32[3,7,128]{2,1,0:T(8,128)S(1)}, f32[3,7,128]{2,1,0:T(8,128)}, u32[]{:S(2)}) copy-start(f32[3,7,128]{2,1,0:T(8,128)} %param.15) | copy-start | bytes 32260
  16.4 363.5 %all-gather.10.cloned.1.call-start = ((), (), s32[]{:S(2)}) async-start(), calls=%async_computation.2 | async-start | bytes 16908288 | tf_op jit(solution)/shard_map/all_gather | solution.py:20
  18.0 48.5 %collective-permute-start.2 = (bf16[6,8192]{1,0:T(8,128)(2,1)}, bf16[6,8192]{1,0:T(8,128)(2,1)S(1)}, u32[]{:S(2)}, u32[]{:S(2)}) collective-permute-start(bf16[6,8192]{1,0:T(8,128)(2,1)} %slice.600), channel_id=1, source_target_pairs={{0,1},{1,2},{2,3},{3,4},{4,5},{5,6},{6,7},{7,8},{8,9},{9,10},{10,1... | collective-permute-start | bytes 294920 | tf_op jit(solution)/shard_map/ppermute | solution.py:14
  22.8 42.0 %collective-permute-start.1 = (bf16[6,8192]{1,0:T(8,128)(2,1)}, bf16[6,8192]{1,0:T(8,128)(2,1)}, u32[]{:S(2)}, u32[]{:S(2)}) collective-permute-start(bf16[6,8192]{1,0:T(8,128)(2,1)} %slice.578), channel_id=1, source_target_pairs={{0,1},{1,2},{2,3},{3,4},{4,5},{5,6},{6,7},{7,8},{8,9},{9,10},{10,1... | collective-permute-start | bytes 294920 | tf_op jit(solution)/shard_map/ppermute | solution.py:14
  25.4 37.8 %collective-permute-start = (bf16[6,8192]{1,0:T(8,128)(2,1)}, bf16[6,8192]{1,0:T(8,128)(2,1)}, u32[]{:S(2)}, u32[]{:S(2)}) collective-permute-start(bf16[6,8192]{1,0:T(8,128)(2,1)} %slice.556), channel_id=1, source_target_pairs={{0,1},{1,2},{2,3},{3,4},{4,5},{5,6},{6,7},{7,8},{8,9},{9,10},{10,1... | collective-permute-start | bytes 294920 | tf_op jit(solution)/shard_map/ppermute | solution.py:14
  41.9 25.2 %copy-start.15 = (f32[8192]{0:T(1024)}, f32[8192]{0:T(1024)S(1)}, u32[]{:S(2)}) copy-start(f32[8192]{0:T(1024)S(1)} %broadcast_in_dim.214) | copy-start | bytes 98308
  42.1 25.0 %copy-start.17 = (f32[8192]{0:T(1024)}, f32[8192]{0:T(1024)S(1)}, u32[]{:S(2)}) copy-start(f32[8192]{0:T(1024)S(1)} %broadcast_in_dim.202) | copy-start | bytes 98308
  42.4 24.7 %copy-start.19 = (f32[8192]{0:T(1024)}, f32[8192]{0:T(1024)S(1)}, u32[]{:S(2)}) copy-start(f32[8192]{0:T(1024)S(1)} %broadcast_in_dim.212) | copy-start | bytes 98308
  42.7 24.4 %copy-start.21 = (f32[8192]{0:T(1024)}, f32[8192]{0:T(1024)S(1)}, u32[]{:S(2)}) copy-start(f32[8192]{0:T(1024)S(1)} %broadcast_in_dim.210) | copy-start | bytes 98308
  43.0 24.2 %copy-start.23 = (f32[8192]{0:T(1024)}, f32[8192]{0:T(1024)S(1)}, u32[]{:S(2)}) copy-start(f32[8192]{0:T(1024)S(1)} %broadcast_in_dim.208) | copy-start | bytes 98308
  43.3 23.9 %copy-start.25 = (f32[8192]{0:T(1024)}, f32[8192]{0:T(1024)S(1)}, u32[]{:S(2)}) copy-start(f32[8192]{0:T(1024)S(1)} %broadcast_in_dim.206) | copy-start | bytes 98308
  43.5 23.6 %copy-start.27 = (f32[8192]{0:T(1024)}, f32[8192]{0:T(1024)S(1)}, u32[]{:S(2)}) copy-start(f32[8192]{0:T(1024)S(1)} %broadcast_in_dim.204) | copy-start | bytes 98308
  43.8 23.4 %copy-start.29 = (f32[8192]{0:T(1024)}, f32[8192]{0:T(1024)S(1)}, u32[]{:S(2)}) copy-start(f32[8192]{0:T(1024)S(1)} %broadcast_in_dim.200) | copy-start | bytes 98308
  44.1 23.1 %copy-start.31 = (f32[8192]{0:T(1024)}, f32[8192]{0:T(1024)S(1)}, u32[]{:S(2)}) copy-start(f32[8192]{0:T(1024)S(1)} %broadcast_in_dim.198) | copy-start | bytes 98308
  44.4 22.8 %copy-start.33 = (f32[8192]{0:T(1024)}, f32[8192]{0:T(1024)S(1)}, u32[]{:S(2)}) copy-start(f32[8192]{0:T(1024)S(1)} %broadcast_in_dim.196) | copy-start | bytes 98308
  44.7 22.6 %copy-start.35 = (f32[8192]{0:T(1024)}, f32[8192]{0:T(1024)S(1)}, u32[]{:S(2)}) copy-start(f32[8192]{0:T(1024)S(1)} %broadcast_in_dim.194) | copy-start | bytes 98308
  44.9 22.3 %copy-start.37 = (f32[8192]{0:T(1024)}, f32[8192]{0:T(1024)S(1)}, u32[]{:S(2)}) copy-start(f32[8192]{0:T(1024)S(1)} %broadcast_in_dim.192) | copy-start | bytes 98308
  45.2 22.0 %copy-start.39 = (f32[8192]{0:T(1024)}, f32[8192]{0:T(1024)S(1)}, u32[]{:S(2)}) copy-start(f32[8192]{0:T(1024)S(1)} %broadcast_in_dim.190) | copy-start | bytes 98308
  45.5 21.8 %copy-start.41 = (f32[8192]{0:T(1024)}, f32[8192]{0:T(1024)S(1)}, u32[]{:S(2)}) copy-start(f32[8192]{0:T(1024)S(1)} %broadcast_in_dim.188) | copy-start | bytes 98308
  45.8 21.5 %copy-start.43 = (f32[8192]{0:T(1024)}, f32[8192]{0:T(1024)S(1)}, u32[]{:S(2)}) copy-start(f32[8192]{0:T(1024)S(1)} %broadcast_in_dim.184) | copy-start | bytes 98308
  46.0 21.2 %copy-start.45 = (f32[8192]{0:T(1024)}, f32[8192]{0:T(1024)S(1)}, u32[]{:S(2)}) copy-start(f32[8192]{0:T(1024)S(1)} %broadcast_in_dim.182) | copy-start | bytes 98308
  48.7 16.1 %copy-start.12 = (bf16[128,8192]{1,0:T(8,128)(2,1)S(1)}, bf16[128,8192]{1,0:T(8,128)(2,1)}, u32[]{:S(2)}) copy-start(bf16[128,8192]{1,0:T(8,128)(2,1)} %param.13) | copy-start | bytes 6291460
  68.1 26.8 %copy-start.53 = (f32[8,2048]{1,0:T(8,128)S(1)}, f32[8,2048]{1,0:T(8,128)}, u32[]{:S(2)}) copy-start(f32[8,2048]{1,0:T(8,128)} %param.18) | copy-start | bytes 196612
  93.5 591.2 %all-gather.8.cloned.1.call-start = ((), (), s32[]{:S(2)}) async-start(), calls=%async_computation.1 | async-start | bytes 16908288 | tf_op jit(solution)/shard_map/all_gather | solution.py:20
  94.8 971.9 %all-gather.12.cloned.1.call-start = ((), (), s32[]{:S(2)}) async-start(), calls=%async_computation.3 | async-start | bytes 33816576 | tf_op jit(solution)/shard_map/all_gather | solution.py:221
  109.9 175.4 %collective-permute-start.3 = (bf16[128,8192]{1,0:T(8,128)(2,1)}, bf16[128,8192]{1,0:T(8,128)(2,1)}, u32[]{:S(2)}, u32[]{:S(2)}) collective-permute-start(bf16[128,8192]{1,0:T(8,128)(2,1)} %get-tuple-element.404), channel_id=1, source_target_pairs={{0,1},{1,2},{2,3},{3,4},{4,5},{5,6},{6,7},{7,8},{8,9},{9,10},{10,1... | collective-permute-start | bytes 6291464 | tf_op jit(solution)/shard_map/ppermute | solution.py:14
  275.4 54.1 %collective-permute-start.5 = (bf16[128,8192]{1,0:T(8,128)(2,1)S(1)}, bf16[128,8192]{1,0:T(8,128)(2,1)}, u32[]{:S(2)}, u32[]{:S(2)}) collective-permute-start(bf16[128,8192]{1,0:T(8,128)(2,1)S(1)} %get-tuple-element.402), channel_id=1, source_target_pairs={{1,0},{2,1},{3,2},{4,3},{5,4},{6,5},{7,6},{8,7},{9,8},{10,9},{11,1... | collective-permute-start | bytes 6291464 | tf_op jit(solution)/shard_map/ppermute | solution.py:14
  280.8 15.7 %copy-start.2 = (f32[129,8192]{1,0:T(8,128)}, f32[129,8192]{1,0:T(8,128)S(1)}, u32[]{:S(2)}) copy-start(f32[129,8192]{1,0:T(8,128)S(1)} %convolution_negate_fusion.1) | copy-start | bytes 12681220
  328.1 8.7 slice-start.2
  342.8 18.9 %copy-start.9 = (f32[129,8192]{1,0:T(8,128)S(1)}, f32[129,8192]{1,0:T(8,128)}, u32[]{:S(2)}) copy-start(f32[129,8192]{1,0:T(8,128)} %fusion.3) | copy-start | bytes 12681220
  379.8 608.9 %copy-start.55 = (f32[1,8192]{1,0:T(1,128)S(1)}, f32[1,8192]{1,0:T(1,128)}, u32[]{:S(2)}) copy-start(f32[1,8192]{1,0:T(1,128)} %copy-done.54) | copy-start | bytes 98308
  379.8 608.9 %copy-start.57 = (f32[1,8192]{1,0:T(1,128)S(1)}, f32[1,8192]{1,0:T(1,128)}, u32[]{:S(2)}) copy-start(f32[1,8192]{1,0:T(1,128)} %copy-done.56) | copy-start | bytes 98308
  379.8 608.9 %copy-start.59 = (f32[1,8192]{1,0:T(1,128)S(1)}, f32[1,8192]{1,0:T(1,128)}, u32[]{:S(2)}) copy-start(f32[1,8192]{1,0:T(1,128)} %copy-done.58) | copy-start | bytes 98308
  379.9 608.9 %copy-start.61 = (f32[1,8192]{1,0:T(1,128)S(1)}, f32[1,8192]{1,0:T(1,128)}, u32[]{:S(2)}) copy-start(f32[1,8192]{1,0:T(1,128)} %copy-done.60) | copy-start | bytes 98308
  379.9 608.9 %copy-start.63 = (f32[1,8192]{1,0:T(1,128)S(1)}, f32[1,8192]{1,0:T(1,128)}, u32[]{:S(2)}) copy-start(f32[1,8192]{1,0:T(1,128)} %copy-done.62) | copy-start | bytes 98308
  379.9 608.9 %copy-start.65 = (f32[1,8192]{1,0:T(1,128)S(1)}, f32[1,8192]{1,0:T(1,128)}, u32[]{:S(2)}) copy-start(f32[1,8192]{1,0:T(1,128)} %copy-done.64) | copy-start | bytes 98308
  379.9 608.9 %copy-start.67 = (f32[1,8192]{1,0:T(1,128)S(1)}, f32[1,8192]{1,0:T(1,128)}, u32[]{:S(2)}) copy-start(f32[1,8192]{1,0:T(1,128)} %copy-done.66) | copy-start | bytes 98308
  379.9 608.9 %copy-start.69 = (f32[1,8192]{1,0:T(1,128)S(1)}, f32[1,8192]{1,0:T(1,128)}, u32[]{:S(2)}) copy-start(f32[1,8192]{1,0:T(1,128)} %copy-done.68) | copy-start | bytes 98308
  379.9 608.9 %copy-start.71 = (f32[128]{0:T(128)S(1)}, f32[128]{0:T(128)}, u32[]{:S(2)}) copy-start(f32[128]{0:T(128)} %iota_add_fusion) | copy-start | bytes 1540
  684.7 333.0 %slice-start = ((s8[4456448]{0:T(1024)(128)(4,1)}), s8[262144]{0:T(1024)(128)(4,1)S(1)}, s32[]{:S(2)}) async-start(s8[4456448]{0:T(1024)(128)(4,1)} %bitcast.138), calls=%async_computation.4 | async-start | bytes 524288
  988.8 29.0 %slice-start.1 = ((s8[4456448]{0:T(1024)(128)(4,1)}), s8[4194304]{0:T(1024)(128)(4,1)S(1)}, s32[]{:S(2)}) async-start(s8[4456448]{0:T(1024)(128)(4,1)} %bitcast.138), calls=%async_computation.5 | async-start | bytes 8388608
  1014.6 33.2 %collective-permute-start.4 = (bf16[6,8192]{1,0:T(8,128)(2,1)S(1)}, bf16[6,8192]{1,0:T(8,128)(2,1)S(1)}, u32[]{:S(2)}, u32[]{:S(2)}) collective-permute-start(bf16[6,8192]{1,0:T(8,128)(2,1)S(1)} %slice.766), channel_id=1, source_target_pairs={{1,0},{2,1},{3,2},{4,3},{5,4},{6,5},{7,6},{8,7},{9,8},{10,9},{11,1... | collective-permute-start | bytes 294920 | tf_op jit(solution)/shard_map/ppermute | solution.py:14
  1041.0 11.0 %collective-permute-start.6 = (bf16[6,8192]{1,0:T(8,128)(2,1)S(1)}, bf16[6,8192]{1,0:T(8,128)(2,1)S(1)}, u32[]{:S(2)}, u32[]{:S(2)}) collective-permute-start(bf16[6,8192]{1,0:T(8,128)(2,1)S(1)} %slice.774), channel_id=1, source_target_pairs={{1,0},{2,1},{3,2},{4,3},{5,4},{6,5},{7,6},{8,7},{9,8},{10,9},{11,1... | collective-permute-start | bytes 294920 | tf_op jit(solution)/shard_map/ppermute | solution.py:14
  1044.7 6.9 collective-permute-start.7
  1066.7 12.7 %copy-start.1 = (f32[128,128]{1,0:T(8,128)S(1)}, f32[128,128]{1,0:T(8,128)}, u32[]{:S(2)}) copy-start(f32[128,128]{1,0:T(8,128)} %param.16) | copy-start | bytes 196612
  (40 other events, 161.9 us)
Sparse Core Ops, SparseCore 0:
  16.5 93.9 all-gather.5
  113.6 91.8 all-gather.9
  208.7 82.1 all-gather.7
  328.2 106.1 all-gather.11
